TPU v7x, 128 devices: a whole 4x4x4 slice. The times are simulated.
128 devices in a mesh: segment: 4 (over x_lo, core), fsdp: 8 (over z, x_hi), dp: 4 (over y).
Axes of the slice: x: 4 (x_hi: 2, x_lo: 2; x = x_hi * 2 + x_lo), y: 4, z: 4, core: 2. Of those that a mesh axis runs over, the one named last changes fastest.
Arguments:
- inputs: bfloat16 [3, 64, 49, 2880], P(None, ('fsdp', 'dp')), may hold values from -6 to 6
- cotangent: bfloat16 [3, 64, 49, 2880], P(None, ('fsdp', 'dp')), may hold values from -0.119628906 to 0.119628906
- plan: int32 [3], replicated, may hold values from 0 to 2, each once
- weight: bfloat16 [4, 2880, 2880], P('segment', 'fsdp'), may hold values from -0.109375 to 0.109375
- squeeze: bfloat16 [4, 2880, 360], P('segment', 'fsdp'), may hold values from -0.109375 to 0.109375
- excite: bfloat16 [4, 2880, 360], P('segment', 'fsdp'), may hold values from -0.3125 to 0.3125
Outputs:
- grad_weight: float32 [4, 2880, 2880], P('segment', ('fsdp', 'dp'))
- grad_squeeze: float32 [4, 2880, 360], P('segment', ('fsdp', 'dp'))
- grad_excite: float32 [4, 2880, 360], P('segment', ('fsdp', 'dp'))
Inputs may be any that keep to these rules, and one draw needn't show every extreme that they name: plan names each of the 3 microbatches exactly once.
All inputs are finite; a program needn't handle non-finite values.
Results may differ from a plain program's by a relative error of at most 0.024.
Values may be sent and summed in bfloat16 or wider, within the bound.
A program may use at most 128 MiB of HBM per device.

v0:
```python
import jax
import jax.numpy as jnp
from jax import lax
from jax.sharding import PartitionSpec as P


def shifted(value, axis, steps):
    count = lax.axis_size(axis)
    leading, last = (max(0, -steps), min(count, count - steps))
    return lax.ppermute(value, axis, [(source, source + steps) for source in range(leading, last)])


def silu_slope(value):
    sigma = jax.nn.sigmoid(value)
    return sigma * (1.0 + value * (1.0 - sigma))


def contract_rows(left, right):
    return lax.dot_general(
        left, right, (((0,), (0,)), ((), ())), preferred_element_type=jnp.float32
    )


def contract_cols(left, right):
    return lax.dot_general(
        left, right, (((1,), (1,)), ((), ())), preferred_element_type=jnp.float32
    )


def project(images, matrix):
    flat = images.reshape(-1, images.shape[-1])
    result = jnp.dot(flat, matrix, preferred_element_type=jnp.float32)
    return result.reshape(images.shape[:-1] + (matrix.shape[1],))


def forward_block(images, matrix, squeeze_w, excite_w):
    pre = project(images, matrix)
    active_map = jax.nn.silu(pre).astype(jnp.bfloat16)
    pooled = jnp.mean(active_map.astype(jnp.float32), axis=1).astype(jnp.bfloat16)
    squeezed = jnp.dot(pooled, squeeze_w, preferred_element_type=jnp.float32)
    hidden = jax.nn.silu(squeezed).astype(jnp.bfloat16)
    gate = jax.nn.sigmoid(contract_cols(hidden, excite_w))
    output = (
        images.astype(jnp.float32) + active_map.astype(jnp.float32) * gate[:, None, :]
    ).astype(jnp.bfloat16)
    return (output, pre, pooled, squeezed, hidden, gate)


def backward_block(images, pre, squeezed, gate, upstream, matrix, squeeze_w, excite_w):
    active_map = jax.nn.silu(pre).astype(jnp.bfloat16)
    upper = upstream.astype(jnp.float32)
    d_act = upper * gate[:, None, :]
    d_gate = jnp.sum(upper * active_map.astype(jnp.float32), axis=1)
    d_excite = (d_gate * gate * (1.0 - gate)).astype(jnp.bfloat16)
    d_hidden = jnp.dot(d_excite, excite_w, preferred_element_type=jnp.float32)
    d_squeezed = (d_hidden * silu_slope(squeezed)).astype(jnp.bfloat16)
    d_pooled = contract_cols(d_squeezed, squeeze_w)
    d_act = d_act + d_pooled[:, None, :] / images.shape[1]
    d_pre = (d_act * silu_slope(pre)).astype(jnp.bfloat16)
    flat = d_pre.reshape(-1, d_pre.shape[-1])
    back = contract_cols(flat, matrix).reshape(images.shape)
    d_images = (upper + back).astype(jnp.bfloat16)
    return (d_excite, d_squeezed, d_pre, d_images)


def put_slot(store, position, value, active):
    current = lax.dynamic_index_in_dim(store, position, 0, keepdims=False)
    return lax.dynamic_update_index_in_dim(store, jnp.where(active, value, current), position, 0)


def take_slot(store, position):
    return lax.dynamic_index_in_dim(store, position, 0, keepdims=False)


def on_device(inputs, cotangent, plan, weight, squeeze, excite):
    full_w, full_s, full_e = (
        lax.all_gather(weight[0], "fsdp", axis=0, tiled=True),
        lax.all_gather(squeeze[0], "fsdp", axis=0, tiled=True),
        lax.all_gather(excite[0], "fsdp", axis=0, tiled=True),
    )
    sections = lax.axis_size("segment")
    segment_id = lax.axis_index("segment")
    ordered = inputs[plan]
    micro, images, pixels, width = ordered.shape
    hidden_width = full_s.shape[1]
    steps_total = micro + sections - 1
    store_in = jnp.zeros((micro, images, pixels, width), jnp.bfloat16)
    store_pre = jnp.zeros((micro, images, pixels, width), jnp.float32)
    store_pool = jnp.zeros((micro, images, width), jnp.bfloat16)
    store_sq = jnp.zeros((micro, images, hidden_width), jnp.float32)
    store_hid = jnp.zeros((micro, images, hidden_width), jnp.bfloat16)
    store_gate = jnp.zeros((micro, images, width), jnp.float32)
    incoming = jnp.zeros((images, pixels, width), jnp.bfloat16)
    for step in range(steps_total):
        slot_now = step - segment_id
        active = (slot_now >= 0) & (slot_now < micro)
        position = jnp.clip(slot_now, 0, micro - 1)
        first_in = ordered[min(step, micro - 1)]
        images_in = jnp.where(segment_id == 0, first_in, incoming)
        output, pre, pooled, squeezed, hidden, gate = forward_block(
            images_in, full_w, full_s, full_e
        )
        store_in = put_slot(store_in, position, images_in, active)
        store_pre = put_slot(store_pre, position, pre, active)
        store_pool = put_slot(store_pool, position, pooled, active)
        store_sq = put_slot(store_sq, position, squeezed, active)
        store_hid = put_slot(store_hid, position, hidden, active)
        store_gate = put_slot(store_gate, position, gate, active)
        if step < steps_total - 1:
            incoming = shifted(output, "segment", 1)
    store_dpre = jnp.zeros((micro, images, pixels, width), jnp.bfloat16)
    store_dsq = jnp.zeros((micro, images, hidden_width), jnp.bfloat16)
    store_dex = jnp.zeros((micro, images, width), jnp.bfloat16)
    incoming_grad = jnp.zeros((images, pixels, width), jnp.bfloat16)
    for step in range(steps_total):
        slot_now = micro - 1 - step + (sections - 1 - segment_id)
        active = (slot_now >= 0) & (slot_now < micro)
        position = jnp.clip(slot_now, 0, micro - 1)
        last_in = cotangent[max(micro - 1 - step, 0)]
        upstream = jnp.where(segment_id == sections - 1, last_in, incoming_grad)
        images_in = take_slot(store_in, position)
        pre = take_slot(store_pre, position)
        squeezed = take_slot(store_sq, position)
        gate = take_slot(store_gate, position)
        d_excite, d_squeezed, d_pre, d_images = backward_block(
            images_in, pre, squeezed, gate, upstream, full_w, full_s, full_e
        )
        store_dpre = put_slot(store_dpre, position, d_pre, active)
        store_dsq = put_slot(store_dsq, position, d_squeezed, active)
        store_dex = put_slot(store_dex, position, d_excite, active)
        if step < steps_total - 1:
            incoming_grad = shifted(d_images, "segment", -1)
    flat_in = store_in.reshape(-1, width)
    flat_dpre = store_dpre.reshape(-1, width)
    grad_s = contract_rows(store_pool.reshape(-1, width), store_dsq.reshape(-1, hidden_width))
    grad_e = contract_rows(store_dex.reshape(-1, width), store_hid.reshape(-1, hidden_width))
    grad_w = contract_rows(flat_in, flat_dpre)
    shard_w, shard_s, shard_e = (
        lax.psum_scatter(
            grad_w.astype(jnp.bfloat16), ("fsdp", "dp"), scatter_dimension=0, tiled=True
        ).astype(jnp.float32),
        lax.psum_scatter(
            grad_s.astype(jnp.bfloat16), ("fsdp", "dp"), scatter_dimension=0, tiled=True
        ).astype(jnp.float32),
        lax.psum_scatter(
            grad_e.astype(jnp.bfloat16), ("fsdp", "dp"), scatter_dimension=0, tiled=True
        ).astype(jnp.float32),
    )
    return (shard_w[None], shard_s[None], shard_e[None])


def solution(mesh):
    placed = (
        P(None, ("fsdp", "dp"), None, None),
        P(None, ("fsdp", "dp"), None, None),
        P(),
        P("segment", "fsdp", None),
        P("segment", "fsdp", None),
        P("segment", "fsdp", None),
    )
    return jax.shard_map(
        on_device,
        mesh=mesh,
        in_specs=placed,
        out_specs=(
            P("segment", ("fsdp", "dp"), None),
            P("segment", ("fsdp", "dp"), None),
            P("segment", ("fsdp", "dp"), None),
        ),
        check_vma=False,
    )
```

profile of v0, /device:TPU:42, one launch (start us, length us, event | category | flops | bytes accessed | tf_op | source)
XLA Modules:
  0.0 888.6 jit_solution(14493084215448957604)
XLA Ops:
  9.5 6.0 gather_fusion
  25.6 168.4 %all-gather.7.cloned.1.call-done = bf16[1,2880,2880]{2,1,0:T(8,128)(2,1)} async-done(((bf16[1,360,2880]{2,1,0:T(8,128)(2,1)}), bf16[1,2880,2880]{2,1,0:T(8,128)(2,1)}) %all-gather.7.cloned.1.call-update) | async-done | bytes 16588816 | tf_op jit(solution)/shard_map/all_gather | solution.py:77
  194.0 9.7 %convert_reduce_fusion.4 = (f32[2,2880]{1,0:T(2,128)S(1)}, bf16[2,49,2880]{2,1,0:T(8,128)(2,1)S(1)}, f32[2,49,2880]{2,1,0:T(8,128)}) fusion(bf16[1,2880,2880]{2,1,0:T(8,128)(2,1)} %all-gather.7.cloned.1.call-done, bf16[1,2,49,2880]{3,1,2,0:T(2,128)(2,1)S(1)} %get-tuple-element.33, pred[]{:T(512)S(6)} %eq.4), kind=kOutput, calls=%fused_computation.130 | convolution fusion | flops 1627954560 | bytes 18869760 | tf_op jit(solution)/shard_map/dot_general | solution.py:32
  203.7 45.0 %all-gather.9.cloned.1.call-done = bf16[1,2880,360]{2,1,0:T(8,128)(2,1)} async-done(((bf16[1,360,360]{2,1,0:T(8,128)(2,1)}), bf16[1,2880,360]{2,1,0:T(8,128)(2,1)}) %all-gather.9.cloned.1.call-update) | async-done | bytes 2073616 | tf_op jit(solution)/shard_map/all_gather | solution.py:78
  250.7 52.7 %all-gather.11.cloned.1.call-done = bf16[1,2880,360]{2,1,0:T(8,128)(2,1)} async-done(((bf16[1,360,360]{2,1,0:T(8,128)(2,1)}), bf16[1,2880,360]{2,1,0:T(8,128)(2,1)}) %all-gather.11.cloned.1.call-update) | async-done | bytes 2073616 | tf_op jit(solution)/shard_map/all_gather | solution.py:79
  310.2 7.3 collective-permute-done
  317.5 8.8 convert_reduce_fusion.3
  335.2 5.6 collective-permute-done.1
  351.4 6.3 collective-permute-done.2
  368.2 6.6 collective-permute-done.3
  385.3 5.7 collective-permute-done.4
  391.0 5.0 bitcast_dynamic-update-slice_fusion
  404.0 12.6 %fusion.54 = bf16[2,49,2880]{2,1,0:T(8,128)(2,1)} fusion(bf16[1,2880,2880]{2,1,0:T(8,128)(2,1)} %all-gather.7.cloned.1.call-done, f32[3,2,49,2880]{3,2,1,0:T(8,128)} %copy-done.9, s32[]{:T(128)S(6)} %min.30, f32[2,2880]{1,0:T(2,128)} %convolution_multiply_fusion.5, f32[2,2880]{1,0:T(2,128)} %copy-done.39, bf16[1,2,49,2880]{3,1,2,0:T(2,128)(2,1)} %get-tuple-element.30, ...), kind=kOutput, calls=%fused_computation.37 | convolution fusion | flops 1630500480 | bytes 20043520 | tf_op jit(solution)/shard_map/dot_general | solution.py:25
  431.9 12.4 %fusion.51 = bf16[2,49,2880]{2,1,0:T(8,128)(2,1)} fusion(bf16[1,2880,2880]{2,1,0:T(8,128)(2,1)} %all-gather.7.cloned.1.call-done, bf16[2,49,2880]{2,0,1:T(2,128)(2,1)} %copy-done.24, bf16[1,2,49,2880]{3,1,2,0:T(2,128)(2,1)S(1)} %copy-done.14, pred[]{:T(512)S(6)} %eq.5, f32[3,2,49,2880]{3,2,1,0:T(8,128)} %copy-done.9, s32[]{:T(128)S(6)} %min.29, ...), kind=kOutput, calls=%fused_computation.36 | convolution fusion | flops 1630500480 | bytes 21197568 | tf_op jit(solution)/shard_map/dot_general | solution.py:25
  461.2 12.2 %fusion.48 = bf16[2,49,2880]{2,1,0:T(8,128)(2,1)} fusion(bf16[1,2880,2880]{2,1,0:T(8,128)(2,1)} %all-gather.7.cloned.1.call-done, bf16[2,49,2880]{2,0,1:T(2,128)(2,1)S(1)} %copy-done.27, bf16[1,2,49,2880]{3,1,2,0:T(2,128)(2,1)S(1)} %get-tuple-element.28, pred[]{:T(512)S(6)} %eq.5, f32[3,2,49,2880]{3,2,1,0:T(8,128)} %copy-done.9, s32[]{:T(128)S(6)} %min.28, ...), kind=kOutput, calls=%fused_computation.35 | convolution fusion | flops 1630500480 | bytes 21197568 | tf_op jit(solution)/shard_map/dot_general | solution.py:25
  490.4 12.2 %fusion.45 = bf16[2,49,2880]{2,1,0:T(8,128)(2,1)} fusion(bf16[1,2880,2880]{2,1,0:T(8,128)(2,1)} %all-gather.7.cloned.1.call-done, bf16[2,49,2880]{2,0,1:T(2,128)(2,1)S(1)} %copy-done.31, bf16[1,2,49,2880]{3,1,2,0:T(2,128)(2,1)S(1)} %get-tuple-element.28, pred[]{:T(512)S(6)} %eq.5, f32[3,2,49,2880]{3,2,1,0:T(8,128)} %copy-done.9, s32[]{:T(128)S(6)} %min.27, ...), kind=kOutput, calls=%fused_computation.34 | convolution fusion | flops 1630500480 | bytes 21197568 | tf_op jit(solution)/shard_map/dot_general | solution.py:25
  519.6 12.2 %fusion.42 = bf16[2,49,2880]{2,1,0:T(8,128)(2,1)} fusion(bf16[1,2880,2880]{2,1,0:T(8,128)(2,1)} %all-gather.7.cloned.1.call-done, bf16[2,49,2880]{2,0,1:T(2,128)(2,1)S(1)} %collective-permute-done.8, bf16[1,2,49,2880]{3,1,2,0:T(2,128)(2,1)S(1)} %get-tuple-element.28, pred[]{:T(512)S(6)} %eq.5, f32[3,2,49,2880]{3,2,1,0:T(8,128)} %copy-done.9, s32[]{:T(128)S(6)} %min.26, ...), kind=kOutput, calls=%fused_computation.33 | convolution fusion | flops 1630500480 | bytes 21197568 | tf_op jit(solution)/shard_map/dot_general | solution.py:25
  553.4 13.9 %bitcast_convert_fusion = bf16[2880,2880]{1,0:T(8,128)(2,1)} fusion(bf16[3,2,49,2880]{3,2,1,0:T(8,128)(2,1)} %bitcast_dynamic-update-slice_fusion.11, bf16[3,2,49,2880]{3,2,1,0:T(8,128)(2,1)S(1)} %bitcast_dynamic-update-slice_fusion.6), kind=kOutput, calls=%fused_computation.1 | convolution fusion | flops 4885401600 | bytes 19975680 | tf_op jit(solution)/shard_map/dot_general | solution.py:19
  567.3 249.8 %fusion.355 = (bf16[96,2880]{1,0:T(8,128)(2,1)S(1)}, bf16[96,360]{1,0:T(8,128)(2,1)S(1)}, bf16[96,360]{1,0:T(8,128)(2,1)S(1)}) fusion(bf16[2880,2880]{1,0:T(8,128)(2,1)} %bitcast_convert_fusion, bf16[2880,360]{1,0:T(8,128)(2,1)} %fusion.25, bf16[2880,360]{1,0:T(8,128)(2,1)S(1)} %copy-done.33), kind=kCustom, calls=%all-reduce-scatter.3 | all-reduce-scatter fusion | flops 11059201 | bytes 21427712
  819.2 5.6 collective-permute-start.11
  830.6 7.7 collective-permute-start.12
  838.2 18.1 %collective-permute-done.15 = bf16[90,360]{1,0:T(8,128)(2,1)S(1)} collective-permute-done((bf16[90,360]{1,0:T(8,128)(2,1)S(1)}, bf16[90,360]{1,0:T(8,128)(2,1)S(1)}, u32[]{:S(2)}, u32[]{:S(2)}) %collective-permute-start.15) | collective-permute-done | bytes 64832
  859.8 7.6 collective-permute-done.13
  868.9 9.5 %concatenate = bf16[282,2880]{1,0:T(8,128)(2,1)} concatenate(bf16[90,2880]{1,0:T(8,128)(2,1)S(1)} %collective-permute-done.11, bf16[96,2880]{1,0:T(8,128)(2,1)S(1)} %collective-permute-done.10, bf16[96,2880]{1,0:T(8,128)(2,1)S(1)} %get-tuple-element.15), dimensions={0} | concatenate | bytes 3248640
  (269 shorter events, 172.5 us)
Async XLA Ops:
  7.2 186.8 %all-gather.7.cloned.1.call-start = ((), (), s32[]{:S(2)}) async-start(), calls=%async_computation | async-start | bytes 19077120 | tf_op jit(solution)/shard_map/all_gather | solution.py:77
  7.9 240.7 %all-gather.9.cloned.1.call-start = ((), (), s32[]{:S(2)}) async-start(), calls=%async_computation.1 | async-start | bytes 2488320 | tf_op jit(solution)/shard_map/all_gather | solution.py:78
  8.7 294.7 %all-gather.11.cloned.1.call-start = ((), (), s32[]{:S(2)}) async-start(), calls=%async_computation.2 | async-start | bytes 2488320 | tf_op jit(solution)/shard_map/all_gather | solution.py:79
  306.4 11.1 %collective-permute-start = (bf16[2,49,2880]{2,0,1:T(2,128)(2,1)S(1)}, bf16[2,49,2880]{2,0,1:T(2,128)(2,1)S(1)}, u32[]{:S(2)}, u32[]{:S(2)}) collective-permute-start(bf16[2,49,2880]{2,0,1:T(2,128)(2,1)S(1)} %copy.44), channel_id=1, source_target_pairs={{0,32},{32,64},{64,96},{1,33},{33,65},{65,97},{2,34},{34,66},{66,9... | collective-permute-start | bytes 1693448 | tf_op jit(solution)/shard_map/ppermute | solution.py:10
  317.5 23.2 %slice-start = ((s8[16957440]{0:T(1024)(128)(4,1)}), s8[4194304]{0:T(1024)(128)(4,1)S(1)}, s32[]{:S(2)}) async-start(s8[16957440]{0:T(1024)(128)(4,1)} %bitcast.890), calls=%async_computation.3 | async-start | bytes 8388608
  317.5 23.2 %slice-start.1 = ((s8[16957440]{0:T(1024)(128)(4,1)}), s8[4194304]{0:T(1024)(128)(4,1)S(1)}, s32[]{:S(2)}) async-start(s8[16957440]{0:T(1024)(128)(4,1)} %bitcast.890), calls=%async_computation.4 | async-start | bytes 8388608
  317.5 23.2 %slice-start.2 = ((s8[16957440]{0:T(1024)(128)(4,1)}), s8[4194304]{0:T(1024)(128)(4,1)S(1)}, s32[]{:S(2)}) async-start(s8[16957440]{0:T(1024)(128)(4,1)} %bitcast.890), calls=%async_computation.5 | async-start | bytes 8388608
  326.4 14.4 %slice-start.3 = ((s8[16957440]{0:T(1024)(128)(4,1)}), s8[4194304]{0:T(1024)(128)(4,1)S(1)}, s32[]{:S(2)}) async-start(s8[16957440]{0:T(1024)(128)(4,1)} %bitcast.890), calls=%async_computation.6 | async-start | bytes 8388608
  329.7 11.1 %collective-permute-start.1 = (bf16[2,49,2880]{2,0,1:T(2,128)(2,1)S(1)}, bf16[2,49,2880]{2,0,1:T(2,128)(2,1)S(1)}, u32[]{:S(2)}, u32[]{:S(2)}) collective-permute-start(bf16[2,49,2880]{2,0,1:T(2,128)(2,1)S(1)} %copy.47), channel_id=1, source_target_pairs={{0,32},{32,64},{64,96},{1,33},{33,65},{65,97},{2,34},{34,66},{66,9... | collective-permute-start | bytes 1693448 | tf_op jit(solution)/shard_map/ppermute | solution.py:10
  346.7 11.1 %collective-permute-start.2 = (bf16[2,49,2880]{2,0,1:T(2,128)(2,1)S(1)}, bf16[2,49,2880]{2,0,1:T(2,128)(2,1)S(1)}, u32[]{:S(2)}, u32[]{:S(2)}) collective-permute-start(bf16[2,49,2880]{2,0,1:T(2,128)(2,1)S(1)} %copy.49), channel_id=1, source_target_pairs={{0,32},{32,64},{64,96},{1,33},{33,65},{65,97},{2,34},{34,66},{66,9... | collective-permute-start | bytes 1693448 | tf_op jit(solution)/shard_map/ppermute | solution.py:10
  363.7 11.1 %collective-permute-start.3 = (bf16[2,49,2880]{2,0,1:T(2,128)(2,1)S(1)}, bf16[2,49,2880]{2,0,1:T(2,128)(2,1)S(1)}, u32[]{:S(2)}, u32[]{:S(2)}) collective-permute-start(bf16[2,49,2880]{2,0,1:T(2,128)(2,1)S(1)} %copy.51), channel_id=1, source_target_pairs={{0,32},{32,64},{64,96},{1,33},{33,65},{65,97},{2,34},{34,66},{66,9... | collective-permute-start | bytes 1693448 | tf_op jit(solution)/shard_map/ppermute | solution.py:10
  379.9 11.2 %collective-permute-start.4 = (bf16[2,49,2880]{2,0,1:T(2,128)(2,1)S(1)}, bf16[2,49,2880]{2,0,1:T(2,128)(2,1)}, u32[]{:S(2)}, u32[]{:S(2)}) collective-permute-start(bf16[2,49,2880]{2,0,1:T(2,128)(2,1)S(1)} %copy.53), channel_id=1, source_target_pairs={{0,32},{32,64},{64,96},{1,33},{33,65},{65,97},{2,34},{34,66},{66,9... | collective-permute-start | bytes 1693448 | tf_op jit(solution)/shard_map/ppermute | solution.py:10
  418.2 9.2 %collective-permute-start.5 = (bf16[2,49,2880]{2,0,1:T(2,128)(2,1)S(1)}, bf16[2,49,2880]{2,0,1:T(2,128)(2,1)S(1)}, u32[]{:S(2)}, u32[]{:S(2)}) collective-permute-start(bf16[2,49,2880]{2,0,1:T(2,128)(2,1)S(1)} %copy.57), channel_id=1, source_target_pairs={{32,0},{64,32},{96,64},{33,1},{65,33},{97,65},{34,2},{66,34},{98,6... | collective-permute-start | bytes 1693448 | tf_op jit(solution)/shard_map/ppermute | solution.py:10
  446.0 10.9 %collective-permute-start.6 = (bf16[2,49,2880]{2,0,1:T(2,128)(2,1)S(1)}, bf16[2,49,2880]{2,0,1:T(2,128)(2,1)S(1)}, u32[]{:S(2)}, u32[]{:S(2)}) collective-permute-start(bf16[2,49,2880]{2,0,1:T(2,128)(2,1)S(1)} %copy.60), channel_id=1, source_target_pairs={{32,0},{64,32},{96,64},{33,1},{65,33},{97,65},{34,2},{66,34},{98,6... | collective-permute-start | bytes 1693448 | tf_op jit(solution)/shard_map/ppermute | solution.py:10
  475.0 11.1 %collective-permute-start.7 = (bf16[2,49,2880]{2,0,1:T(2,128)(2,1)S(1)}, bf16[2,49,2880]{2,0,1:T(2,128)(2,1)S(1)}, u32[]{:S(2)}, u32[]{:S(2)}) collective-permute-start(bf16[2,49,2880]{2,0,1:T(2,128)(2,1)S(1)} %copy.62), channel_id=1, source_target_pairs={{32,0},{64,32},{96,64},{33,1},{65,33},{97,65},{34,2},{66,34},{98,6... | collective-permute-start | bytes 1693448 | tf_op jit(solution)/shard_map/ppermute | solution.py:10
  504.2 11.1 %collective-permute-start.8 = (bf16[2,49,2880]{2,0,1:T(2,128)(2,1)S(1)}, bf16[2,49,2880]{2,0,1:T(2,128)(2,1)S(1)}, u32[]{:S(2)}, u32[]{:S(2)}) collective-permute-start(bf16[2,49,2880]{2,0,1:T(2,128)(2,1)S(1)} %copy.64), channel_id=1, source_target_pairs={{32,0},{64,32},{96,64},{33,1},{65,33},{97,65},{34,2},{66,34},{98,6... | collective-permute-start | bytes 1693448 | tf_op jit(solution)/shard_map/ppermute | solution.py:10
  533.4 11.1 %collective-permute-start.9 = (bf16[2,49,2880]{2,0,1:T(2,128)(2,1)S(1)}, bf16[2,49,2880]{2,0,1:T(2,128)(2,1)S(1)}, u32[]{:S(2)}, u32[]{:S(2)}) collective-permute-start(bf16[2,49,2880]{2,0,1:T(2,128)(2,1)S(1)} %copy.66), channel_id=1, source_target_pairs={{32,0},{64,32},{96,64},{33,1},{65,33},{97,65},{34,2},{66,34},{98,6... | collective-permute-start | bytes 1693448 | tf_op jit(solution)/shard_map/ppermute | solution.py:10
  567.3 262.0 %copy-start.44 = (u32[128]{0:T(128)S(1)}, u32[128]{0:T(128)}, u32[]{:S(2)}) copy-start(u32[128]{0:T(128)} %constant.371) | copy-start | bytes 1540
  817.1 51.8 %collective-permute-start.10 = (bf16[96,2880]{1,0:T(8,128)(2,1)S(1)}, bf16[96,2880]{1,0:T(8,128)(2,1)S(1)}, u32[]{:S(2)}, u32[]{:S(2)}) collective-permute-start(bf16[96,2880]{1,0:T(8,128)(2,1)S(1)} %get-tuple-element.15), channel_id=1, source_target_pairs={{0,1},{1,2},{2,3},{3,4},{4,5},{5,6},{6,7},{7,8},{8,9},{9,10},{10,1... | collective-permute-start | bytes 1658888
  819.2 49.7 %collective-permute-start.11 = (bf16[90,2880]{1,0:T(8,128)(2,1)S(1)}, bf16[90,2880]{1,0:T(8,128)(2,1)S(1)}, u32[]{:S(2)}, u32[]{:S(2)}) collective-permute-start(bf16[90,2880]{1,0:T(8,128)(2,1)S(1)} %slice.35), channel_id=1, source_target_pairs={{0,2},{1,3},{2,4},{3,5},{4,6},{5,7},{6,8},{7,9},{8,10},{9,11},{10,... | collective-permute-start | bytes 1555208
  824.8 33.4 %collective-permute-start.14 = (bf16[96,360]{1,0:T(8,128)(2,1)S(1)}, bf16[96,360]{1,0:T(8,128)(2,1)S(1)}, u32[]{:S(2)}, u32[]{:S(2)}) collective-permute-start(bf16[96,360]{1,0:T(8,128)(2,1)S(1)} %get-tuple-element.17), channel_id=1, source_target_pairs={{0,1},{1,2},{2,3},{3,4},{4,5},{5,6},{6,7},{7,8},{8,9},{9,10},{10,1... | collective-permute-start | bytes 207368
  826.8 29.6 %collective-permute-start.15 = (bf16[90,360]{1,0:T(8,128)(2,1)S(1)}, bf16[90,360]{1,0:T(8,128)(2,1)S(1)}, u32[]{:S(2)}, u32[]{:S(2)}) collective-permute-start(bf16[90,360]{1,0:T(8,128)(2,1)S(1)} %slice.37), channel_id=1, source_target_pairs={{0,2},{1,3},{2,4},{3,5},{4,6},{5,7},{6,8},{7,9},{8,10},{9,11},{10,... | collective-permute-start | bytes 194408
  830.6 36.8 %collective-permute-start.12 = (bf16[96,360]{1,0:T(8,128)(2,1)S(1)}, bf16[96,360]{1,0:T(8,128)(2,1)S(1)}, u32[]{:S(2)}, u32[]{:S(2)}) collective-permute-start(bf16[96,360]{1,0:T(8,128)(2,1)S(1)} %get-tuple-element.16), channel_id=1, source_target_pairs={{0,1},{1,2},{2,3},{3,4},{4,5},{5,6},{6,7},{7,8},{8,9},{9,10},{10,1... | collective-permute-start | bytes 207368
  856.3 11.0 %collective-permute-start.13 = (bf16[90,360]{1,0:T(8,128)(2,1)S(1)}, bf16[90,360]{1,0:T(8,128)(2,1)S(1)}, u32[]{:S(2)}, u32[]{:S(2)}) collective-permute-start(bf16[90,360]{1,0:T(8,128)(2,1)S(1)} %slice.36), channel_id=1, source_target_pairs={{0,2},{1,3},{2,4},{3,5},{4,6},{5,7},{6,8},{7,9},{8,10},{9,11},{10,... | collective-permute-start | bytes 194408
  (46 other events, 190.3 us)
Sparse Core Ops, SparseCore 0:
  10.3 183.6 all-gather.6
  196.3 52.3 all-gather.8
  251.0 52.3 all-gather.10
where the time goes:
time: 898 us; the launch traced here: 889 us
  waiting for transfers between devices  332 us (37%)
  blocking collectives  250 us (28%)
  matrix products  138 us (15%)
  local copies, waits for them, and re-layouts  65.1 us (7%)
  starting transfers between devices  50.3 us (6%)
  other arithmetic  38.5 us (4%)
  between operations  15.5 us (2%)
    unnamed x1, blocking collectives  250 us
    all_gather x1, waiting for transfers between devices, on_device(): lax.all_gather(weight[0], 'fsdp', axis=0, tiled=True)  168 us
    dot_general x17, matrix products, contract_cols(): lax.dot_general(left, right, (((1,), (1,)), ((), ())), preferred_element_...  74.6 us
    all_gather x1, waiting for transfers between devices, on_device(): lax.all_gather(excite[0], 'fsdp', axis=0, tiled=True)  52.7 us
    all_gather x1, waiting for transfers between devices, on_device(): lax.all_gather(squeeze[0], 'fsdp', axis=0, tiled=True)  45 us
    ppermute x10, waiting for transfers between devices, shifted(): lax.ppermute(value, axis, [(source, source + steps) for source in range(l...  37.8 us
    dot_general x6, matrix products, project(): result = jnp.dot(flat, matrix, preferred_element_type=jnp.float32)  34.4 us
    ppermute x10, starting transfers between devices, shifted(): lax.ppermute(value, axis, [(source, source + steps) for source in range(l...  28.7 us
  transfers between devices with their start and end apart: 19, of which 15 were waited for; matrix products, arithmetic and copies ran while one was open for 8% of the time, Pallas kernels for 0%

commit v1 on v0

--- a/solution.py
+++ b/solution.py
@@ -2,6 +2,16 @@
 import jax.numpy as jnp
 from jax import lax
 from jax.sharding import PartitionSpec as P
+
+_meet_local_data = lambda my_data, which_axis: jnp.concatenate(
+    jax.lax.all_to_all(
+        jnp.stack([my_data] * jax.lax.axis_size(which_axis)),
+        axis_name=which_axis,
+        split_axis=0,
+        concat_axis=0,
+    ),
+    axis=0,
+)
 
 
 def shifted(value, axis, steps):
@@ -74,7 +84,7 @@
 
 def on_device(inputs, cotangent, plan, weight, squeeze, excite):
     full_w, full_s, full_e = (
-        lax.all_gather(weight[0], "fsdp", axis=0, tiled=True),
+        _meet_local_data(weight[0], "fsdp"),
         lax.all_gather(squeeze[0], "fsdp", axis=0, tiled=True),
         lax.all_gather(excite[0], "fsdp", axis=0, tiled=True),
     )

time: 898 us -> 891 us (level)
  waiting for transfers between devices: 332 us -> 295 us
  matrix products: 138 us -> 157 us
    all_to_all x0 -> x1, waiting for transfers between devices: none -> 183 us  [jax.lax.all_to_all(jnp.stack([my_data] * jax.lax.axis_size(which_axis)),...]
    all_gather x1 -> x0, waiting for transfers between devices: 168 us -> none  [on_device(): lax.all_gather(weight[0], 'fsdp', axis=0, tiled=True)]
    all_gather x1, waiting for transfers between devices: 45 us -> 0.02 us  [on_device(): lax.all_gather(squeeze[0], 'fsdp', axis=0, tiled=True)]
    dot_general x6, matrix products: 34.4 us -> 53.2 us  [project(): result = jnp.dot(flat, matrix, preferred_element_type=jnp.float32)]
    unnamed x9 -> x8, waiting for transfers between devices: 27.7 us -> 27 us
    unnamed x112 -> x100, local copies, waits for them, and re-layouts: 20.5 us -> 20.1 us
  transfers between devices with their start and end apart: 19 -> 19, of which waited for: 15 -> 14; matrix products, arithmetic and copies ran while one was open for 8% -> 8% of each run, Pallas kernels for 0% -> 0%
where the time goes in v1:
time: 891 us; the launch traced here: 881 us
  waiting for transfers between devices  295 us (33%)
  blocking collectives  250 us (28%)
  matrix products  157 us (18%)
  local copies, waits for them, and re-layouts  71.7 us (8%)
  starting transfers between devices  57.6 us (6%)
  other arithmetic  34.6 us (4%)
  between operations  15.8 us (2%)
    unnamed x1, blocking collectives  250 us
    all_to_all x1, waiting for transfers between devices, jax.lax.all_to_all(jnp.stack([my_data] * jax.lax.axis_size(which_axis)),...  183 us
    dot_general x17, matrix products, contract_cols(): lax.dot_general(left, right, (((1,), (1,)), ((), ())), preferred_element_...  74.6 us
    dot_general x6, matrix products, project(): result = jnp.dot(flat, matrix, preferred_element_type=jnp.float32)  53.2 us
    all_gather x1, waiting for transfers between devices, on_device(): lax.all_gather(excite[0], 'fsdp', axis=0, tiled=True)  45.7 us
    ppermute x10, waiting for transfers between devices, shifted(): lax.ppermute(value, axis, [(source, source + steps) for source in range(l...  39.2 us
    ppermute x10, starting transfers between devices, shifted(): lax.ppermute(value, axis, [(source, source + steps) for source in range(l...  28.9 us
    unnamed x8, waiting for transfers between devices  27 us
  transfers between devices with their start and end apart: 19, of which 14 were waited for; matrix products, arithmetic and copies ran while one was open for 8% of the time, Pallas kernels for 0%

profile of v1, /device:TPU:42, one launch (start us, length us, event | category | flops | bytes accessed | tf_op | source)
XLA Modules:
  0.0 881.4 jit_solution(6184647605714641634)
XLA Ops:
  7.2 7.3 stack.3
  14.5 7.1 all-to-all-start
  39.1 183.4 %all-to-all-done = bf16[8,360,2880]{2,1,0:T(8,128)(2,1)} async-done(((bf16[8,360,2880]{2,1,0:T(8,128)(2,1)}), bf16[8,360,2880]{2,1,0:T(8,128)(2,1)}, u32[]{:S(2)}, u32[]{:S(2)}) %all-to-all-start) | async-done | bytes 16588832 | tf_op jit(solution)/shard_map/all_to_all | solution.py:7
  222.5 9.7 %convert_reduce_fusion.4 = (f32[2,2880]{1,0:T(2,128)S(1)}, bf16[2,49,2880]{2,1,0:T(8,128)(2,1)S(1)}, f32[2,49,2880]{2,1,0:T(8,128)}) fusion(bf16[2880,2880,1]{1,0,2:T(8,128)(2,1)} %bitcast.4, bf16[1,2,49,2880]{3,1,2,0:T(2,128)(2,1)S(1)} %get-tuple-element.33, pred[]{:T(512)S(6)} %eq.4), kind=kOutput, calls=%fused_computation.107 | convolution fusion | flops 1627954560 | bytes 18869760 | tf_op jit(solution)/shard_map/dot_general | solution.py:42
  234.2 45.7 %all-gather.7.cloned.1.call-done = bf16[1,2880,360]{2,1,0:T(8,128)(2,1)} async-done(((bf16[1,360,360]{2,1,0:T(8,128)(2,1)}), bf16[1,2880,360]{2,1,0:T(8,128)(2,1)}) %all-gather.7.cloned.1.call-update) | async-done | bytes 2073616 | tf_op jit(solution)/shard_map/all_gather | solution.py:89
  286.7 7.3 collective-permute-done
  294.1 8.8 convert_reduce_fusion.3
  317.0 8.7 convert_reduce_fusion.2
  332.3 6.4 collective-permute-done.2
  338.7 8.7 convert_reduce_fusion.1
  353.8 6.5 collective-permute-done.3
  360.3 8.7 convert_reduce_fusion
  382.3 8.8 bitcast_dynamic-update-slice_fusion
  396.7 12.4 %fusion.5 = bf16[2,49,2880]{2,1,0:T(8,128)(2,1)} fusion(bf16[2880,2880,1]{1,0,2:T(8,128)(2,1)} %bitcast.4, bf16[1,2,49,2880]{3,1,2,0:T(2,128)(2,1)} %get-tuple-element.30, pred[]{:T(512)S(6)} %eq.5, f32[3,2,49,2880]{3,2,1,0:T(8,128)} %copy-done.9, s32[]{:T(128)S(6)} %min.30, f32[2,2880]{1,0:T(2,128)} %convolution_multiply_fusion.5, ...), kind=kOutput, calls=%fused_computation.11 | convolution fusion | flops 1630500480 | bytes 20043520 | tf_op jit(solution)/shard_map/dot_general | solution.py:35
  424.3 12.4 %fusion.6 = bf16[2,49,2880]{2,1,0:T(8,128)(2,1)} fusion(bf16[2880,2880,1]{1,0,2:T(8,128)(2,1)} %bitcast.4, bf16[2,49,2880]{2,0,1:T(2,128)(2,1)} %copy-done.26, bf16[1,2,49,2880]{3,1,2,0:T(2,128)(2,1)S(1)} %copy-done.14, pred[]{:T(512)S(6)} %eq.5, f32[3,2,49,2880]{3,2,1,0:T(8,128)} %copy-done.9, s32[]{:T(128)S(6)} %min.29, ...), kind=kOutput, calls=%fused_computation.12 | convolution fusion | flops 1630500480 | bytes 21197568 | tf_op jit(solution)/shard_map/dot_general | solution.py:35
  453.8 12.2 %fusion.7 = bf16[2,49,2880]{2,1,0:T(8,128)(2,1)} fusion(bf16[2880,2880,1]{1,0,2:T(8,128)(2,1)} %bitcast.4, bf16[2,49,2880]{2,0,1:T(2,128)(2,1)S(1)} %copy-done.29, bf16[1,2,49,2880]{3,1,2,0:T(2,128)(2,1)S(1)} %get-tuple-element.28, pred[]{:T(512)S(6)} %eq.5, f32[3,2,49,2880]{3,2,1,0:T(8,128)} %copy-done.9, s32[]{:T(128)S(6)} %min.28, ...), kind=kOutput, calls=%fused_computation.13 | convolution fusion | flops 1630500480 | bytes 21197568 | tf_op jit(solution)/shard_map/dot_general | solution.py:35
  482.9 12.2 %fusion.8 = bf16[2,49,2880]{2,1,0:T(8,128)(2,1)} fusion(bf16[2880,2880,1]{1,0,2:T(8,128)(2,1)} %bitcast.4, bf16[2,49,2880]{2,0,1:T(2,128)(2,1)S(1)} %copy-done.33, bf16[1,2,49,2880]{3,1,2,0:T(2,128)(2,1)S(1)} %get-tuple-element.28, pred[]{:T(512)S(6)} %eq.5, f32[3,2,49,2880]{3,2,1,0:T(8,128)} %copy-done.9, s32[]{:T(128)S(6)} %min.27, ...), kind=kOutput, calls=%fused_computation.14 | convolution fusion | flops 1630500480 | bytes 21197568 | tf_op jit(solution)/shard_map/dot_general | solution.py:35
  512.2 12.2 %fusion.9 = bf16[2,49,2880]{2,1,0:T(8,128)(2,1)} fusion(bf16[2880,2880,1]{1,0,2:T(8,128)(2,1)} %bitcast.4, bf16[2,49,2880]{2,0,1:T(2,128)(2,1)S(1)} %collective-permute-done.8, bf16[1,2,49,2880]{3,1,2,0:T(2,128)(2,1)S(1)} %get-tuple-element.28, pred[]{:T(512)S(6)} %eq.5, f32[3,2,49,2880]{3,2,1,0:T(8,128)} %copy-done.9, s32[]{:T(128)S(6)} %min.26, ...), kind=kOutput, calls=%fused_computation.15 | convolution fusion | flops 1630500480 | bytes 21197568 | tf_op jit(solution)/shard_map/dot_general | solution.py:35
  546.0 13.9 %bitcast_convert_fusion = bf16[2880,2880]{1,0:T(8,128)(2,1)} fusion(bf16[3,2,49,2880]{3,2,1,0:T(8,128)(2,1)} %bitcast_dynamic-update-slice_fusion.11, bf16[3,2,49,2880]{3,2,1,0:T(8,128)(2,1)S(1)} %bitcast_dynamic-update-slice_fusion.6), kind=kOutput, calls=%fused_computation.1 | convolution fusion | flops 4885401600 | bytes 19975680 | tf_op jit(solution)/shard_map/dot_general | solution.py:29
  559.9 249.8 %fusion.303 = (bf16[96,2880]{1,0:T(8,128)(2,1)S(1)}, bf16[96,360]{1,0:T(8,128)(2,1)S(1)}, bf16[96,360]{1,0:T(8,128)(2,1)S(1)}) fusion(bf16[2880,2880]{1,0:T(8,128)(2,1)} %bitcast_convert_fusion, bf16[2880,360]{1,0:T(8,128)(2,1)} %fusion.3, bf16[2880,360]{1,0:T(8,128)(2,1)S(1)} %copy-done.35), kind=kCustom, calls=%all-reduce-scatter.3 | all-reduce-scatter fusion | flops 11059201 | bytes 21427712
  823.2 7.7 collective-permute-start.12
  830.8 18.0 %collective-permute-done.15 = bf16[90,360]{1,0:T(8,128)(2,1)S(1)} collective-permute-done((bf16[90,360]{1,0:T(8,128)(2,1)S(1)}, bf16[90,360]{1,0:T(8,128)(2,1)S(1)}, u32[]{:S(2)}, u32[]{:S(2)}) %collective-permute-start.15) | collective-permute-done | bytes 64832
  852.3 7.6 collective-permute-done.13
  861.4 9.5 %concatenate = bf16[282,2880]{1,0:T(8,128)(2,1)} concatenate(bf16[90,2880]{1,0:T(8,128)(2,1)S(1)} %collective-permute-done.11, bf16[96,2880]{1,0:T(8,128)(2,1)S(1)} %collective-permute-done.10, bf16[96,2880]{1,0:T(8,128)(2,1)S(1)} %get-tuple-element.15), dimensions={0} | concatenate | bytes 3248640
  (256 shorter events, 180.7 us)
Async XLA Ops:
  7.2 16.0 %copy-start = (bf16[3,2,49,2880]{3,1,2,0:T(2,128)(2,1)S(1)}, bf16[3,2,49,2880]{3,1,2,0:T(2,128)(2,1)}, u32[]{:S(2)}) copy-start(bf16[3,2,49,2880]{3,1,2,0:T(2,128)(2,1)} %param.6) | copy-start | bytes 5080324
  14.5 208.0 %all-to-all-start = ((bf16[8,360,2880]{2,1,0:T(8,128)(2,1)}), bf16[8,360,2880]{2,1,0:T(8,128)(2,1)}, u32[]{:S(2)}, u32[]{:S(2)}) async-start(bf16[8,360,2880]{2,1,0:T(8,128)(2,1)} %stack.3), calls=%async_computation | async-start | bytes 33914880 | tf_op jit(solution)/shard_map/all_to_all | solution.py:7
  21.6 210.6 %all-gather.5.cloned.1.call-start = ((), (), s32[]{:S(2)}) async-start(), calls=%async_computation.1 | async-start | bytes 2488320 | tf_op jit(solution)/shard_map/all_gather | solution.py:88
  22.3 257.6 %all-gather.7.cloned.1.call-start = ((), (), s32[]{:S(2)}) async-start(), calls=%async_computation.2 | async-start | bytes 2488320 | tf_op jit(solution)/shard_map/all_gather | solution.py:89
  283.0 11.1 %collective-permute-start = (bf16[2,49,2880]{2,0,1:T(2,128)(2,1)S(1)}, bf16[2,49,2880]{2,0,1:T(2,128)(2,1)S(1)}, u32[]{:S(2)}, u32[]{:S(2)}) collective-permute-start(bf16[2,49,2880]{2,0,1:T(2,128)(2,1)S(1)} %copy.44), channel_id=1, source_target_pairs={{0,32},{32,64},{64,96},{1,33},{33,65},{65,97},{2,34},{34,66},{66,9... | collective-permute-start | bytes 1693448 | tf_op jit(solution)/shard_map/ppermute | solution.py:20
  294.1 8.8 %copy-start.2 = (bf16[1,2880,360]{2,1,0:T(8,128)(2,1)S(1)}, bf16[1,2880,360]{2,1,0:T(8,128)(2,1)}, u32[]{:S(2)}) copy-start(bf16[1,2880,360]{2,1,0:T(8,128)(2,1)} %all-gather.5.cloned.1.call-done) | copy-start | bytes 6220804
  306.0 11.1 %collective-permute-start.1 = (bf16[2,49,2880]{2,0,1:T(2,128)(2,1)S(1)}, bf16[2,49,2880]{2,0,1:T(2,128)(2,1)S(1)}, u32[]{:S(2)}, u32[]{:S(2)}) collective-permute-start(bf16[2,49,2880]{2,0,1:T(2,128)(2,1)S(1)} %copy.47), channel_id=1, source_target_pairs={{0,32},{32,64},{64,96},{1,33},{33,65},{65,97},{2,34},{34,66},{66,9... | collective-permute-start | bytes 1693448 | tf_op jit(solution)/shard_map/ppermute | solution.py:20
  327.6 11.1 %collective-permute-start.2 = (bf16[2,49,2880]{2,0,1:T(2,128)(2,1)S(1)}, bf16[2,49,2880]{2,0,1:T(2,128)(2,1)S(1)}, u32[]{:S(2)}, u32[]{:S(2)}) collective-permute-start(bf16[2,49,2880]{2,0,1:T(2,128)(2,1)S(1)} %copy.49), channel_id=1, source_target_pairs={{0,32},{32,64},{64,96},{1,33},{33,65},{65,97},{2,34},{34,66},{66,9... | collective-permute-start | bytes 1693448 | tf_op jit(solution)/shard_map/ppermute | solution.py:20
  349.3 11.1 %collective-permute-start.3 = (bf16[2,49,2880]{2,0,1:T(2,128)(2,1)S(1)}, bf16[2,49,2880]{2,0,1:T(2,128)(2,1)S(1)}, u32[]{:S(2)}, u32[]{:S(2)}) collective-permute-start(bf16[2,49,2880]{2,0,1:T(2,128)(2,1)S(1)} %copy.51), channel_id=1, source_target_pairs={{0,32},{32,64},{64,96},{1,33},{33,65},{65,97},{2,34},{34,66},{66,9... | collective-permute-start | bytes 1693448 | tf_op jit(solution)/shard_map/ppermute | solution.py:20
  371.2 11.1 %collective-permute-start.4 = (bf16[2,49,2880]{2,0,1:T(2,128)(2,1)S(1)}, bf16[2,49,2880]{2,0,1:T(2,128)(2,1)S(1)}, u32[]{:S(2)}, u32[]{:S(2)}) collective-permute-start(bf16[2,49,2880]{2,0,1:T(2,128)(2,1)S(1)} %copy.53), channel_id=1, source_target_pairs={{0,32},{32,64},{64,96},{1,33},{33,65},{65,97},{2,34},{34,66},{66,9... | collective-permute-start | bytes 1693448 | tf_op jit(solution)/shard_map/ppermute | solution.py:20
  376.6 14.4 %copy-start.15 = (bf16[1,2,49,2880]{3,1,2,0:T(2,128)(2,1)S(1)}, bf16[1,2,49,2880]{3,1,2,0:T(2,128)(2,1)}, u32[]{:S(2)}) copy-start(bf16[1,2,49,2880]{3,1,2,0:T(2,128)(2,1)} %get-tuple-element.30) | copy-start | bytes 1693444
  410.8 9.2 %collective-permute-start.5 = (bf16[2,49,2880]{2,0,1:T(2,128)(2,1)S(1)}, bf16[2,49,2880]{2,0,1:T(2,128)(2,1)S(1)}, u32[]{:S(2)}, u32[]{:S(2)}) collective-permute-start(bf16[2,49,2880]{2,0,1:T(2,128)(2,1)S(1)} %copy.57), channel_id=1, source_target_pairs={{32,0},{64,32},{96,64},{33,1},{65,33},{97,65},{34,2},{66,34},{98,6... | collective-permute-start | bytes 1693448 | tf_op jit(solution)/shard_map/ppermute | solution.py:20
  438.3 11.1 %collective-permute-start.6 = (bf16[2,49,2880]{2,0,1:T(2,128)(2,1)S(1)}, bf16[2,49,2880]{2,0,1:T(2,128)(2,1)S(1)}, u32[]{:S(2)}, u32[]{:S(2)}) collective-permute-start(bf16[2,49,2880]{2,0,1:T(2,128)(2,1)S(1)} %copy.60), channel_id=1, source_target_pairs={{32,0},{64,32},{96,64},{33,1},{65,33},{97,65},{34,2},{66,34},{98,6... | collective-permute-start | bytes 1693448 | tf_op jit(solution)/shard_map/ppermute | solution.py:20
  467.6 11.0 %collective-permute-start.7 = (bf16[2,49,2880]{2,0,1:T(2,128)(2,1)S(1)}, bf16[2,49,2880]{2,0,1:T(2,128)(2,1)S(1)}, u32[]{:S(2)}, u32[]{:S(2)}) collective-permute-start(bf16[2,49,2880]{2,0,1:T(2,128)(2,1)S(1)} %copy.62), channel_id=1, source_target_pairs={{32,0},{64,32},{96,64},{33,1},{65,33},{97,65},{34,2},{66,34},{98,6... | collective-permute-start | bytes 1693448 | tf_op jit(solution)/shard_map/ppermute | solution.py:20
  496.8 11.1 %collective-permute-start.8 = (bf16[2,49,2880]{2,0,1:T(2,128)(2,1)S(1)}, bf16[2,49,2880]{2,0,1:T(2,128)(2,1)S(1)}, u32[]{:S(2)}, u32[]{:S(2)}) collective-permute-start(bf16[2,49,2880]{2,0,1:T(2,128)(2,1)S(1)} %copy.64), channel_id=1, source_target_pairs={{32,0},{64,32},{96,64},{33,1},{65,33},{97,65},{34,2},{66,34},{98,6... | collective-permute-start | bytes 1693448 | tf_op jit(solution)/shard_map/ppermute | solution.py:20
  526.1 11.1 %collective-permute-start.9 = (bf16[2,49,2880]{2,0,1:T(2,128)(2,1)S(1)}, bf16[2,49,2880]{2,0,1:T(2,128)(2,1)S(1)}, u32[]{:S(2)}, u32[]{:S(2)}) collective-permute-start(bf16[2,49,2880]{2,0,1:T(2,128)(2,1)S(1)} %copy.66), channel_id=1, source_target_pairs={{32,0},{64,32},{96,64},{33,1},{65,33},{97,65},{34,2},{66,34},{98,6... | collective-permute-start | bytes 1693448 | tf_op jit(solution)/shard_map/ppermute | solution.py:20
  546.0 13.9 %copy-start.35 = (bf16[2880,360]{1,0:T(8,128)(2,1)S(1)}, bf16[2880,360]{1,0:T(8,128)(2,1)}, u32[]{:S(2)}) copy-start(bf16[2880,360]{1,0:T(8,128)(2,1)} %fusion.4) | copy-start | bytes 6220804
  559.9 262.0 %copy-start.43 = (u32[128]{0:T(128)S(1)}, u32[128]{0:T(128)}, u32[]{:S(2)}) copy-start(u32[128]{0:T(128)} %constant.371) | copy-start | bytes 1540
  809.7 51.7 %collective-permute-start.10 = (bf16[96,2880]{1,0:T(8,128)(2,1)S(1)}, bf16[96,2880]{1,0:T(8,128)(2,1)S(1)}, u32[]{:S(2)}, u32[]{:S(2)}) collective-permute-start(bf16[96,2880]{1,0:T(8,128)(2,1)S(1)} %get-tuple-element.15), channel_id=1, source_target_pairs={{0,1},{1,2},{2,3},{3,4},{4,5},{5,6},{6,7},{7,8},{8,9},{9,10},{10,1... | collective-permute-start | bytes 1658888
  811.8 49.6 %collective-permute-start.11 = (bf16[90,2880]{1,0:T(8,128)(2,1)S(1)}, bf16[90,2880]{1,0:T(8,128)(2,1)S(1)}, u32[]{:S(2)}, u32[]{:S(2)}) collective-permute-start(bf16[90,2880]{1,0:T(8,128)(2,1)S(1)} %slice.35), channel_id=1, source_target_pairs={{0,2},{1,3},{2,4},{3,5},{4,6},{5,7},{6,8},{7,9},{8,10},{9,11},{10,... | collective-permute-start | bytes 1555208
  817.4 33.4 %collective-permute-start.14 = (bf16[96,360]{1,0:T(8,128)(2,1)S(1)}, bf16[96,360]{1,0:T(8,128)(2,1)S(1)}, u32[]{:S(2)}, u32[]{:S(2)}) collective-permute-start(bf16[96,360]{1,0:T(8,128)(2,1)S(1)} %get-tuple-element.17), channel_id=1, source_target_pairs={{0,1},{1,2},{2,3},{3,4},{4,5},{5,6},{6,7},{7,8},{8,9},{9,10},{10,1... | collective-permute-start | bytes 207368
  819.3 29.5 %collective-permute-start.15 = (bf16[90,360]{1,0:T(8,128)(2,1)S(1)}, bf16[90,360]{1,0:T(8,128)(2,1)S(1)}, u32[]{:S(2)}, u32[]{:S(2)}) collective-permute-start(bf16[90,360]{1,0:T(8,128)(2,1)S(1)} %slice.37), channel_id=1, source_target_pairs={{0,2},{1,3},{2,4},{3,5},{4,6},{5,7},{6,8},{7,9},{8,10},{9,11},{10,... | collective-permute-start | bytes 194408
  823.2 36.7 %collective-permute-start.12 = (bf16[96,360]{1,0:T(8,128)(2,1)S(1)}, bf16[96,360]{1,0:T(8,128)(2,1)S(1)}, u32[]{:S(2)}, u32[]{:S(2)}) collective-permute-start(bf16[96,360]{1,0:T(8,128)(2,1)S(1)} %get-tuple-element.16), channel_id=1, source_target_pairs={{0,1},{1,2},{2,3},{3,4},{4,5},{5,6},{6,7},{7,8},{8,9},{9,10},{10,1... | collective-permute-start | bytes 207368
  848.8 11.0 %collective-permute-start.13 = (bf16[90,360]{1,0:T(8,128)(2,1)S(1)}, bf16[90,360]{1,0:T(8,128)(2,1)S(1)}, u32[]{:S(2)}, u32[]{:S(2)}) collective-permute-start(bf16[90,360]{1,0:T(8,128)(2,1)S(1)} %slice.36), channel_id=1, source_target_pairs={{0,2},{1,3},{2,4},{3,5},{4,6},{5,7},{6,8},{7,9},{8,10},{9,11},{10,... | collective-permute-start | bytes 194408
  (40 other events, 155.4 us)
Sparse Core Ops, SparseCore 0:
  24.7 201.0 all-gather.4
  228.2 51.7 all-gather.6
